TPU v7x, 32 devices: a whole 2x2x4 slice. The times are simulated.
32 devices in a mesh: member: 2 (over y), lon: 8 (over z, x), lat: 2 (over core).
Axes of the slice: x: 2, y: 2, z: 4, core: 2. Of those that a mesh axis runs over, the one named last changes fastest.
Arguments:
- fields: bfloat16 [1280, 32, 128], P('member', 'lat', 'lon'), parts along dimension 0, may hold values from -6 to 6
- support_rows: int32 [7, 32, 16], replicated, may hold values from -1 to 1
- support_lons: int32 [7, 32, 16], replicated, may hold values from -64 to 64, as said below
- support_weights: float32 [7, 32, 16], replicated, may hold values from -1.5 to 1.5
- mix_weight: bfloat16 [7, 640, 640], replicated, may hold values from -0.09375 to 0.09375
- norm_gain: float32 [640], replicated, may hold values from 0.1 to 1.9
- up_weight: bfloat16 [640, 1280], replicated, may hold values from -0.25 to 0.25
- down_weight: bfloat16 [1280, 640], replicated, may hold values from -0.15625 to 0.15625
Outputs:
- output: bfloat16 [1280, 32, 128], P('member', 'lat', 'lon'), parts along dimension 0
There are 2 independent parts, one for each index of `member`. A program takes and returns all parts, laid end to end along the dimension named above; an argument that names none is the same for every part. Nothing has to cross between parts.
Inputs may be any that keep to these rules, and one draw needn't show every extreme that they name: `support_lons`: at output row i every offset lies within plus or minus min(64, 4 * 32 // min(i + 1, 32 - i)); in every basis filter the first pole row has an entry at -(64) and the last pole row one at 64.
All inputs are finite; a program needn't handle non-finite values.
Results may differ from a plain program's by a relative error of at most 0.0095.
Values may be sent and summed in bfloat16 or wider, within the bound.
A program may use at most 128 MiB of HBM per device.

v0:
```python
import functools
import math

import jax
import jax.numpy as jnp
from jax import lax
from jax.experimental import pallas as pl
from jax.experimental.pallas import tpu as pltpu
from jax.sharding import PartitionSpec as P

norm_eps = 1e-05
MESH = pl.DeviceIdType.MESH


def plan_copies(lon_count, lat_count, rows, cols):
    lon_total, row_total = lon_count * cols, lat_count * rows

    def reach(row):
        nearest = min(row + 1, row_total - row)
        return min(lon_total // 2, 4 * row_total // nearest)

    def distance(row):
        return min(-(-reach(row) // cols), lon_count // 2)

    def in_half(span, delta):
        if delta == 0 or abs(delta) == lon_count // 2:
            return False
        return span - cols * (abs(delta) - 1) <= cols // 2

    need = [distance(max(p - 1, 0)) for p in range(rows)]
    deltas = [d for d in range(1 - lon_count // 2, lon_count // 2 + 1) if d != 0]
    counts = {delta: sum(1 for d in need if d >= abs(delta)) for delta in deltas}
    spans = [reach(max(p - 1, 0)) for p in range(rows)]
    fulls = {d: sum(1 for p in range(counts[d]) if not in_half(spans[p], d)) for d in deltas}
    edge, edge_span = 0, 0
    for boundary in range(1, lat_count):
        edge = max(edge, distance(boundary * rows - 1), distance(boundary * rows))
        edge_span = max(edge_span, reach(boundary * rows - 1), reach(boundary * rows))
    halo = [d for d in range(1 - lon_count // 2, lon_count // 2 + 1) if abs(d) <= edge]
    groups = [(rows // 2, rows), (rows // 4, rows // 2), (0, rows // 4)]
    stages = []
    upper = rows
    for low, _ in groups:
        lower = max(low - 1, 0)
        stage = []
        for delta in sorted(deltas, key=lambda d: -abs(d)):
            full, top = min(fulls[delta], upper), min(counts[delta], upper)
            if full > lower:
                stage.append(("block", delta, lower, full, False))
            if top > max(full, lower):
                stage.append(("block", delta, max(full, lower), top, True))
        stages.append(stage)
        upper = lower
    if lat_count > 1:
        stages[0] = [
            (side, d, 0, 1, in_half(edge_span, d)) for d in halo for side in ("down", "up")
        ] + stages[0]
    halves = [d for d in halo if in_half(edge_span, d)]
    return groups, stages, counts, fulls, halo, halves


def block_kernel(
    lon_count,
    lat_count,
    plan,
    x_hbm,
    rows_ref,
    lons_ref,
    weights_ref,
    gain_ref,
    mix_hbm,
    up_hbm,
    down_hbm,
    out_hbm,
    x_ref,
    out_ref,
    window,
    filters,
    product,
    mix_ref,
    up_ref,
    down_ref,
    send_sem,
    recv_sem,
    load_sem,
    out_sem,
):
    rows, cols, channels = x_ref.shape
    bases, entries = rows_ref.shape[:2]
    lon_total = lon_count * cols
    middle = lon_count // 2
    groups, stages, counts, fulls, halo, halves = plan
    me, lat = lax.axis_index("lon"), lax.axis_index("lat")
    north = 2 * lat < lat_count
    has_low, has_high = lat > 0, lat < lat_count - 1

    loads = [
        pltpu.make_async_copy(mix_hbm, mix_ref, load_sem.at[0]),
        pltpu.make_async_copy(up_hbm, up_ref, load_sem.at[1]),
        pltpu.make_async_copy(down_hbm, down_ref, load_sem.at[2]),
    ]
    fetch = pltpu.make_async_copy(x_hbm, x_ref, load_sem.at[3])
    fetch.start()

    barrier = pltpu.get_barrier_semaphore()
    halo_deltas = halo if lat_count > 1 else []
    for delta in range(1, lon_count):
        pl.semaphore_signal(
            barrier, inc=1, device_id={"lon": lax.rem(me + delta, lon_count)}, device_id_type=MESH
        )
    for present, other in ((has_low, lat - 1), (has_high, lat + 1)):

        @pl.when(present)
        def _():
            for delta in halo_deltas:
                target = lax.rem(me + lon_count - delta, lon_count)
                pl.semaphore_signal(
                    barrier, inc=1, device_id={"lon": target, "lat": other}, device_id_type=MESH
                )

    sides = jnp.where(has_low, 1, 0) + jnp.where(has_high, 1, 0)
    pl.semaphore_wait(barrier, lon_count - 1 + sides * len(halo_deltas))
    fetch.wait()

    def copy_of(index, item):
        kind, delta, first, last, halved = item
        width = cols // 2 if halved else cols
        offset = cols // 2 if halved and delta < 0 else 0
        target = lax.rem(me + lon_count - delta, lon_count)
        slot = (delta + middle) % lon_count
        here, there = pl.ds(offset, width), pl.ds(slot * cols + offset, width)
        if kind == "block":
            start = jnp.where(north, first, rows - last)
            source = x_ref.at[pl.ds(start, last - first), here]
            landing = window.at[pl.ds(start + 1, last - first), there]
            device = {"lon": target}
        elif kind == "down":
            source = x_ref.at[pl.ds(rows - 1, 1), here]
            landing = window.at[pl.ds(0, 1), there]
            device = {"lon": target, "lat": jnp.minimum(lat + 1, lat_count - 1)}
        else:
            source = x_ref.at[pl.ds(0, 1), here]
            landing = window.at[pl.ds(rows + 1, 1), there]
            device = {"lon": target, "lat": jnp.maximum(lat - 1, 0)}
        return pltpu.make_async_remote_copy(
            src_ref=source,
            dst_ref=landing,
            send_sem=send_sem.at[index],
            recv_sem=recv_sem.at[index],
            device_id=device,
            device_id_type=MESH,
        )

    copies = []
    for stage in stages:
        copies.append(list(enumerate(stage, sum(len(done) for done in copies))))

    def each(items, sending, action):
        for index, item in items:
            if item[0] == "block":
                action(copy_of(index, item))
            else:
                present = has_high if (item[0] == "down") == sending else has_low

                @pl.when(present)
                def _():
                    action(copy_of(index, item))

    for stage in copies:
        each(stage, True, lambda copy: copy.start())
    for load in loads:
        load.start()

    window[1 : rows + 1, middle * cols : (middle + 1) * cols, :] = x_ref[...]
    for delta, count in counts.items():
        slot = (delta + middle) % lon_count
        if count < rows:
            gap = (rows - count, cols, channels)
            window[pl.ds(jnp.where(north, count, 0) + 1, rows - count),
                   slot * cols : (slot + 1) * cols] = jnp.zeros(gap, jnp.bfloat16)
        partial = count - fulls[delta]
        if partial > 0:
            far = slot * cols + (0 if delta < 0 else cols // 2)
            window[pl.ds(jnp.where(north, fulls[delta], rows - count) + 1, partial),
                   far : far + cols // 2] = jnp.zeros(
                (partial, cols // 2, channels), jnp.bfloat16
            )
    for delta in halves:
        far = (delta + middle) % lon_count * cols + (0 if delta < 0 else cols // 2)
        for line in (0, rows + 1):
            window[line, far : far + cols // 2] = jnp.zeros((cols // 2, channels), jnp.bfloat16)
    for present, line in ((has_low, 0), (has_high, rows + 1)):
        for delta in range(1 - middle, middle + 1):
            slot = (delta + middle) % lon_count

            def clear():
                window[line, slot * cols : (slot + 1) * cols] = jnp.zeros(
                    (cols, channels), jnp.bfloat16
                )

            if delta in halo and lat_count > 1:
                pl.when(jnp.logical_not(present))(clear)
            else:
                clear()

    lanes = lax.broadcasted_iota(jnp.int32, (rows, lon_total), 1)
    wide = (rows, rows_ref.shape[2])
    own_rows = (
        lax.broadcasted_iota(jnp.int32, wide, 0) + lat * rows
        == lax.broadcasted_iota(jnp.int32, wide, 1)
    ).astype(jnp.float32)

    def own(ref, k):
        return lax.dot_general(
            own_rows,
            ref[k].astype(jnp.float32),
            (((1,), (1,)), ((), ())),
            precision=lax.Precision.HIGHEST,
            preferred_element_type=jnp.float32,
        )

    def build(k, carry):
        spot = own(lons_ref, k).astype(jnp.int32) + middle * cols
        spot = jnp.where(spot >= lon_total, spot - lon_total, spot)
        row_offset = own(rows_ref, k)
        weight = own(weights_ref, k)
        picked = [jnp.where(row_offset == r, weight, 0.0) for r in (-1.0, 0.0, 1.0)]
        sums = [jnp.zeros((rows, lon_total), jnp.float32) for _ in range(3)]
        for s in range(entries):
            hit = spot[:, s : s + 1] == lanes
            for r in range(3):
                sums[r] = sums[r] + jnp.where(hit, picked[r][:, s : s + 1], 0.0)
        for r in range(3):
            for i in range(rows):
                line = jnp.broadcast_to(sums[r][i : i + 1, :], (cols, lon_total))
                turned = pltpu.roll(line, 0, 1, stride=1, stride_axis=0)
                filters[i, pl.ds(pl.multiple_of(k * cols, cols), cols),
                        r * lon_total : (r + 1) * lon_total] = turned.astype(jnp.bfloat16)
        return carry

    lax.fori_loop(0, bases, build, 0)

    def group(low, high):
        start = jnp.where(north, low, rows - high)
        half = high - low
        lines = half * cols
        def filter_row(t, carry):
            i = start + t
            source = window[pl.ds(i, 3)].reshape(3 * lon_total, channels)
            filtered = jnp.dot(filters[i], source, preferred_element_type=jnp.float32)
            filtered = filtered.astype(jnp.bfloat16)
            at = pl.multiple_of(t * cols, cols)
            for k in range(bases):
                product[pl.ds(at, cols), k * channels : (k + 1) * channels] = filtered[
                    k * cols : (k + 1) * cols
                ]
            return carry

        lax.fori_loop(0, half, filter_row, 0)
        mixed = jnp.dot(product[:lines], mix_ref[...], preferred_element_type=jnp.float32)
        here = x_ref[pl.ds(start, half)].reshape(lines, channels)
        latent = here.astype(jnp.float32) + mixed
        mean = jnp.mean(latent, axis=1, keepdims=True)
        centred = latent - mean
        variance = jnp.mean(centred * centred, axis=1, keepdims=True)
        normed = (centred * lax.rsqrt(variance + norm_eps) * gain_ref[...][None, :]).astype(jnp.bfloat16)
        raised = jnp.dot(normed, up_ref[...], preferred_element_type=jnp.float32)
        hidden = 0.5 * raised * (1.0 + lax.erf(raised * math.sqrt(0.5)))
        lowered = jnp.dot(
            hidden.astype(jnp.bfloat16), down_ref[...], preferred_element_type=jnp.float32
        )
        result = (latent + lowered).astype(jnp.bfloat16)
        out_ref[pl.ds(start, half)] = result.reshape(half, cols, channels)

    puts = []
    for stage, (low, high) in zip(copies, groups):
        each(stage, False, lambda copy: copy.wait_recv())
        if stage is copies[0]:
            for load in loads:
                load.wait()
        group(low, high)
        part = pl.ds(jnp.where(north, low, rows - high), high - low)
        put = pltpu.make_async_copy(out_ref.at[part], out_hbm.at[part], out_sem.at[len(puts)])
        put.start()
        puts.append(put)
    for stage in copies:
        each(stage, True, lambda copy: copy.wait_send())
    for put in puts:
        put.wait()


def source_reach(lon_total, row_total, p):
    row = max(p - 1, 0)
    return min(lon_total // 2, 4 * row_total // min(row + 1, row_total - row))


def relay_fits(lon_count, lat_count, rows, cols):
    lon_total, row_total = lon_count * cols, lat_count * rows
    if lon_count != 8 or lat_count != 2 or rows % 8 != 0 or cols % 16 != 0:
        return False
    return source_reach(lon_total, row_total, rows // 2 + 1) <= cols and lon_total == 128


def relay_kernel(
    lon_count,
    lat_count,
    x_hbm,
    rows_ref,
    lons_ref,
    weights_ref,
    gain_ref,
    mix_hbm,
    up_hbm,
    down_hbm,
    out_ref,
    window,
    wide_filters,
    near_filters,
    product,
    mix_ref,
    up_ref,
    down_ref,
    send_sem,
    recv_sem,
    load_sem,
):
    rows, cols, channels = x_hbm.shape
    bases, entries = rows_ref.shape[:2]
    lon_total, row_total = lon_count * cols, lat_count * rows
    middle, part, half = lon_count // 2, cols // 2, rows // 2
    home = middle * cols
    reaches = [source_reach(lon_total, row_total, p) for p in range(rows)]
    full = sum(1 for r in reaches if r > 2 * cols)
    wide = sum(1 for r in reaches if r > cols + part)
    near = sum(1 for r in reaches if r > cols)
    me, lat = lax.axis_index("lon"), lax.axis_index("lat")
    north = lat == 0
    turn = 1 - 2 * lax.rem(me, 2)
    edge = jnp.where(north, rows - 1, 0)

    def device(delta):
        return lax.rem(me + delta + lon_count, lon_count)

    def at(delta):
        return pl.multiple_of(lax.rem(delta + middle + lon_count, lon_count) * cols, cols)

    def lines(first, last):
        return pl.ds(jnp.where(north, first, rows - last) + 1, last - first)

    fetch = pltpu.make_async_copy(
        x_hbm, window.at[pl.ds(1, rows), pl.ds(home, cols)], load_sem.at[3]
    )
    fetch.start()
    loads = [
        pltpu.make_async_copy(mix_hbm, mix_ref, load_sem.at[0]),
        pltpu.make_async_copy(up_hbm, up_ref, load_sem.at[1]),
        pltpu.make_async_copy(down_hbm, down_ref, load_sem.at[2]),
    ]
    barrier = pltpu.get_barrier_semaphore()
    others = [{"lon": me + turn}] + [{"lon": device(2 * e)} for e in (1, -1, 2)]
    others.append({"lat": 1 - lat})
    for other in others:
        pl.semaphore_signal(barrier, inc=1, device_id=other, device_id_type=MESH)
    for load in loads:
        load.start()

    def clear(where, low, high):
        size = where.size if isinstance(where, pl.Slice) else 1
        window[where, low:high] = jnp.zeros((size, high - low, channels), jnp.bfloat16)

    outer, halo = jnp.where(north, 0, rows + 1), jnp.where(north, rows + 1, 0)
    clear(pl.ds(outer, 1), 0, lon_total)
    clear(lines(full, wide), 0, home - 2 * cols)
    clear(lines(full, wide), home + 3 * cols, lon_total)
    clear(lines(wide, near), 0, home - cols - part)
    clear(lines(wide, near), home + 2 * cols + part, lon_total)
    clear(lines(near, half + 1), 0, home - cols)
    clear(lines(near, half + 1), home + 2 * cols, lon_total)
    clear(lines(half + 1, rows), home + 2 * cols, home + 3 * cols)
    clear(pl.ds(halo, 1), home - cols, home - part)
    clear(pl.ds(halo, 1), home + cols + part, home + 3 * cols)

    count = [0]

    def message(where, here, there, width, target, landing=None):
        index = count[0]
        count[0] += 1
        landing = where if landing is None else landing
        return pltpu.make_async_remote_copy(
            src_ref=window.at[where, pl.ds(here, width)],
            dst_ref=window.at[landing, pl.ds(there, width)],
            send_sem=send_sem.at[index],
            recv_sem=recv_sem.at[index],
            device_id=target,
            device_id_type=MESH,
        )

    partner, beside = {"lon": me + turn}, {"lon": device(2 * turn)}
    core, core_line = {"lat": 1 - lat}, pl.ds(edge + 1, 1)
    core_landing = pl.ds(jnp.where(north, 0, rows + 1), 1)

    def own_across(first, last):
        return message(lines(first, last), home, at(-turn), cols, partner)

    def own_along(first, last, e):
        return message(lines(first, last), home, at(-2 * e), cols, {"lon": device(2 * e)})

    def half_along(first, last, e):
        offset = part if e > 0 else 0
        return message(
            lines(first, last), home + offset, at(-2 * e) + offset, part, {"lon": device(2 * e)}
        )

    def pass_along(first, last):
        return message(lines(first, last), at(turn), at(-turn), cols, beside)

    def pass_across(first, last, e):
        return message(lines(first, last), at(2 * e), at(2 * e - turn), cols, partner)

    def to_core(col, width):
        return message(core_line, col, col, width, core, core_landing)

    after = pl.multiple_of(home + jnp.where(turn > 0, cols, -part), part)
    before = pl.multiple_of(home + jnp.where(turn > 0, -part, cols), part)
    near_cut = half + (rows - half) // 2
    steps = (1, -1, 2)
    halo_own = to_core(home, cols)
    halo_across, halo_along = to_core(after, part), to_core(before, part)
    across = [own_across(near_cut, rows), own_across(half, near_cut), own_across(wide, half)]
    across_wide = own_across(0, wide)
    along = [pass_along(near_cut, rows), pass_along(half, near_cut), pass_along(wide, half)]
    halves = [half_along(wide, near, e) for e in (1, -1)]
    wide_along = {e: own_along(full, wide, e) for e in (1, -1)}
    wide_across = message(lines(full, wide), at(2 * turn), at(turn), cols, partner)
    bands = [(full - 1, full), (1, full - 1), (0, 1)]
    full_along = [[own_along(a, b, e) for e in steps] for a, b in bands]
    full_across = [[pass_across(a, b, e) for e in steps] for a, b in bands]

    def start(*copies):
        for copy in copies:
            copy.start()

    def arrived(*copies):
        for copy in copies:
            copy.wait_recv()

    wide_rows = (half, rows_ref.shape[2])

    def table(ref, k, first):
        order = lax.broadcasted_iota(jnp.int32, wide_rows, 0) + first
        local = jnp.where(north, order, rows - 2 - order + 2 * lax.rem(order, 2))
        mine = (local + lat * rows == lax.broadcasted_iota(jnp.int32, wide_rows, 1)).astype(
            jnp.float32
        )
        return lax.dot_general(
            mine,
            ref[k].astype(jnp.float32),
            (((1,), (1,)), ((), ())),
            precision=lax.Precision.HIGHEST,
            preferred_element_type=jnp.float32,
        )

    lanes = lax.broadcasted_iota(jnp.int32, (half, lon_total), 1)
    second = lax.rem(lax.broadcasted_iota(jnp.int32, (half, entries), 0), 2)

    def turned(line):
        spread = jnp.broadcast_to(line, (cols, lon_total))
        return pltpu.roll(spread, 0, 1, stride=1, stride_axis=0).astype(jnp.bfloat16)

    def build_near(k, carry):
        offset = table(lons_ref, k, half).astype(jnp.int32)
        row_offset = table(rows_ref, k, half).astype(jnp.int32)
        weight = table(weights_ref, k, half)
        spot = (row_offset + 1 + second) * (4 * cols) + offset + cols
        sums = [jnp.zeros((half, lon_total), jnp.float32) for _ in range(2)]
        for s in range(entries):
            for v in range(2):
                hit = spot[:, s : s + 1] == lanes + v * lon_total
                sums[v] = sums[v] + jnp.where(hit, weight[:, s : s + 1], 0.0)
        for n in range(half):
            for v in range(2):
                spot_at = pl.multiple_of(k * 2 * cols + (n % 2) * cols, cols)
                near_filters[n // 2, pl.ds(spot_at, cols), v * lon_total : (v + 1) * lon_total] = (
                    turned(sums[v][n : n + 1, :])
                )
        return carry

    def build_wide(k, carry):
        spot = table(lons_ref, k, 0).astype(jnp.int32) + home
        spot = jnp.where(spot >= lon_total, spot - lon_total, spot)
        row_offset = table(rows_ref, k, 0)
        weight = table(weights_ref, k, 0)
        picked = [jnp.where(row_offset == r, weight, 0.0) for r in (-1.0, 0.0, 1.0)]
        sums = [jnp.zeros((half, lon_total), jnp.float32) for _ in range(3)]
        for s in range(entries):
            hit = spot[:, s : s + 1] == lanes
            for r in range(3):
                sums[r] = sums[r] + jnp.where(hit, picked[r][:, s : s + 1], 0.0)
        for n in range(half):
            late = n % 2
            spot_at = pl.ds(pl.multiple_of(k * 2 * cols + late * cols, cols), cols)
            for r in range(3):
                low = (r + late) * lon_total
                wide_filters[n // 2, spot_at, low : low + lon_total] = turned(sums[r][n : n + 1, :])
            low = (3 - 3 * late) * lon_total
            wide_filters[n // 2, spot_at, low : low + lon_total] = jnp.zeros(
                (cols, lon_total), jnp.bfloat16
            )
        return carry

    def filter_pairs(first, last):
        pairs = last - first
        base = jnp.where(north, 2 * first, rows - 2 * last)
        for t in range(pairs):
            q = jnp.where(north, first + t, last - 1 - t)
            taken = pl.ds(base + 2 * t, 4)
            if 2 * first >= half:
                low = home - cols
                source = window[taken, low : low + 4 * cols].reshape(16 * cols, channels)
                matrix = near_filters[q - half // 2]
            else:
                source = window[taken].reshape(4 * lon_total, channels)
                matrix = wide_filters[q]
            filtered = jnp.dot(matrix, source, preferred_element_type=jnp.float32)
            filtered = filtered.astype(jnp.bfloat16)
            for k in range(bases):
                product[2 * t * cols : 2 * (t + 1) * cols, k * channels : (k + 1) * channels] = (
                    filtered[2 * k * cols : 2 * (k + 1) * cols]
                )

    def finish_pairs(first, last, between=()):
        base = jnp.where(north, 2 * first, rows - 2 * last)
        depth = 2 * (last - first)
        cells = depth * cols
        mixed = jnp.dot(product[:cells], mix_ref[...], preferred_element_type=jnp.float32)
        here = window[pl.ds(base + 1, depth), home : home + cols].reshape(cells, channels)
        latent = here.astype(jnp.float32) + mixed
        mean = jnp.mean(latent, axis=1, keepdims=True)
        centred = latent - mean
        variance = jnp.mean(centred * centred, axis=1, keepdims=True)
        normed = (centred * lax.rsqrt(variance + norm_eps) * gain_ref[...][None, :]).astype(
            jnp.bfloat16
        )
        raised = jnp.dot(normed, up_ref[...], preferred_element_type=jnp.float32)
        hidden = 0.5 * raised * (1.0 + lax.erf(raised * math.sqrt(0.5)))
        lowered = jnp.dot(
            hidden.astype(jnp.bfloat16), down_ref[...], preferred_element_type=jnp.float32
        )
        result = (latent + lowered).astype(jnp.bfloat16)
        out_ref[pl.ds(base, depth)] = result.reshape(depth, cols, channels)

    pl.semaphore_wait(barrier, len(others))
    fetch.wait()
    start(halo_own, *across, across_wide)
    start(*wide_along.values(), *full_along[0])
    lax.fori_loop(0, bases, build_near, 0)
    arrived(across[0])
    start(along[0], halo_across)
    start(*full_along[1])
    lax.fori_loop(0, bases, build_wide, 0)
    arrived(across[1])
    start(along[1])
    arrived(*wide_along.values())
    start(wide_across)
    arrived(*full_along[0])
    start(*full_across[0])
    start(*full_along[2])
    arrived(across[2])
    start(along[2], *halves)
    arrived(along[0])
    start(halo_along)
    for load in loads:
        load.wait()
    quarter = half // 4
    arrived(halo_own, halo_across, halo_along)
    arrived(*full_along[1])
    start(*full_across[1])
    arrived(along[1])
    filter_pairs(3 * quarter, 4 * quarter)
    finish_pairs(3 * quarter, 4 * quarter)
    arrived(*full_along[2])
    start(*full_across[2])
    arrived(along[2], *halves)
    filter_pairs(2 * quarter, 3 * quarter)
    finish_pairs(2 * quarter, 3 * quarter)
    arrived(across_wide, wide_across, *full_across[0])
    filter_pairs(quarter, 2 * quarter)
    finish_pairs(quarter, 2 * quarter)
    arrived(*full_across[1], *full_across[2])
    filter_pairs(0, quarter)
    finish_pairs(0, quarter)
    sent = [halo_own, halo_across, halo_along, across_wide, wide_across]
    sent += across + along + halves + list(wide_along.values())
    for group in full_along + full_across:
        sent += group
    for copy in sent:
        copy.wait_send()


def relay_call(
    lon_count,
    lat_count,
    fields,
    support_rows,
    support_lons,
    support_weights,
    mix_weight,
    norm_gain,
    up_weight,
    down_weight,
):
    channels, rows, cols = fields.shape
    bases, hidden = mix_weight.shape[0], up_weight.shape[1]
    lon_total = lon_count * cols
    half, copies = rows // 2, 36
    in_vmem = pl.BlockSpec(memory_space=pltpu.VMEM)
    anywhere = pl.BlockSpec(memory_space=pl.ANY)
    result = pl.pallas_call(
        functools.partial(relay_kernel, lon_count, lat_count),
        out_shape=pltpu.VMEM((rows, cols, channels), jnp.bfloat16),
        in_specs=[anywhere] + [in_vmem] * 4 + [anywhere] * 3,
        out_specs=in_vmem,
        scratch_shapes=[
            pltpu.VMEM((rows + 2, lon_total, channels), jnp.bfloat16),
            pltpu.VMEM((half // 2, 2 * bases * cols, 4 * lon_total), jnp.bfloat16),
            pltpu.VMEM((half // 2, 2 * bases * cols, 16 * cols), jnp.bfloat16),
            pltpu.VMEM((half * cols, bases * channels), jnp.bfloat16),
            pltpu.VMEM((bases * channels, channels), jnp.bfloat16),
            pltpu.VMEM((channels, hidden), jnp.bfloat16),
            pltpu.VMEM((hidden, channels), jnp.bfloat16),
            pltpu.SemaphoreType.DMA((copies,)),
            pltpu.SemaphoreType.DMA((copies,)),
            pltpu.SemaphoreType.DMA((4,)),
        ],
        compiler_params=pltpu.CompilerParams(
            collective_id=0, has_side_effects=True, vmem_limit_bytes=56 * 1024 * 1024
        ),
    )(
        jnp.transpose(fields, (1, 2, 0)),
        jnp.transpose(support_rows, (0, 2, 1)),
        jnp.transpose(support_lons, (0, 2, 1)),
        jnp.transpose(support_weights, (0, 2, 1)),
        norm_gain,
        mix_weight.reshape(bases * channels, channels),
        up_weight,
        down_weight,
    )
    return jnp.transpose(result, (2, 0, 1))


def direct_call(
    lon_count,
    lat_count,
    fields,
    support_rows,
    support_lons,
    support_weights,
    mix_weight,
    norm_gain,
    up_weight,
    down_weight,
):
    channels, rows, cols = fields.shape
    bases, hidden = mix_weight.shape[0], up_weight.shape[1]
    lon_total = lon_count * cols
    plan = plan_copies(lon_count, lat_count, rows, cols)
    count = sum(len(stage) for stage in plan[1])
    in_vmem = pl.BlockSpec(memory_space=pltpu.VMEM)
    anywhere = pl.BlockSpec(memory_space=pl.ANY)
    result = pl.pallas_call(
        functools.partial(block_kernel, lon_count, lat_count, plan),
        out_shape=jax.ShapeDtypeStruct((rows, cols, channels), jnp.bfloat16),
        in_specs=[anywhere] + [in_vmem] * 4 + [anywhere] * 3,
        out_specs=anywhere,
        scratch_shapes=[
            pltpu.VMEM((rows, cols, channels), jnp.bfloat16),
            pltpu.VMEM((rows, cols, channels), jnp.bfloat16),
            pltpu.VMEM((rows + 2, lon_total, channels), jnp.bfloat16),
            pltpu.VMEM((rows, bases * cols, 3 * lon_total), jnp.bfloat16),
            pltpu.VMEM((rows // 2 * cols, bases * channels), jnp.bfloat16),
            pltpu.VMEM((bases * channels, channels), jnp.bfloat16),
            pltpu.VMEM((channels, hidden), jnp.bfloat16),
            pltpu.VMEM((hidden, channels), jnp.bfloat16),
            pltpu.SemaphoreType.DMA((count,)),
            pltpu.SemaphoreType.DMA((count,)),
            pltpu.SemaphoreType.DMA((4,)),
            pltpu.SemaphoreType.DMA((len(plan[0]),)),
        ],
        compiler_params=pltpu.CompilerParams(
            collective_id=0, has_side_effects=True, vmem_limit_bytes=56 * 1024 * 1024
        ),
    )(
        jnp.transpose(fields, (1, 2, 0)),
        jnp.transpose(support_rows, (0, 2, 1)),
        jnp.transpose(support_lons, (0, 2, 1)),
        jnp.transpose(support_weights, (0, 2, 1)),
        norm_gain,
        mix_weight.reshape(bases * channels, channels),
        up_weight,
        down_weight,
    )
    return jnp.transpose(result, (2, 0, 1))


def on_device(lon_count, lat_count, *arrays):
    channels, rows, cols = arrays[0].shape
    if relay_fits(lon_count, lat_count, rows, cols):
        return relay_call(lon_count, lat_count, *arrays)
    return direct_call(lon_count, lat_count, *arrays)


def solution(mesh):
    in_specs = (P("member", "lat", "lon"), P(), P(), P(), P(), P(), P(), P())
    out_specs = P("member", "lat", "lon")
    return jax.shard_map(
        functools.partial(on_device, mesh.shape["lon"], mesh.shape["lat"]),
        mesh=mesh,
        in_specs=in_specs,
        out_specs=out_specs,
        check_vma=False,
    )
```

profile of v0, /device:TPU:0, one launch (start us, length us, event | category | flops | bytes accessed | tf_op | source)
XLA Modules:
  0.0 30.7 jit_solution(16826401187539122610)
XLA Ops:
  0.0 30.0 %shard_map.82 = bf16[16,16,640]{2,1,0:T(8,128)(2,1)S(1)} custom-call(bf16[16,16,640]{2,1,0:T(8,128)(2,1)} %bitcast.8, s32[7,16,32]{2,1,0:T(8,128)} %bitcast.9, s32[7,16,32]{2,1,0:T(8,128)} %bitcast.10, f32[7,16,32]{2,1,0:T(8,128)} %bitcast.11, f32[640]{0:T(1024)} %gain_ref.1, bf16[4480,640]{1,0:T(8,128)(2,1)} %bitcast.7, bf16[640,1280]{1,0:T(8,128)(2,1)} %up_hbm.1, ...), custom_call_target="tpu_custom_call" | custom-call | tf_op jit(solution)/shard_map/pallas_call | solution.py:618
  30.0 0.7 %copy.10 = bf16[640,16,16]{0,2,1:T(8,128)(2,1)} copy(bf16[640,16,16]{0,2,1:T(8,128)(2,1)S(1)} %bitcast.6) | data formatting | bytes 655360
where the time goes:
time: 30.9 us; the launch traced here: 30.7 us
  Pallas kernels  30 us (97%)
  local copies, waits for them, and re-layouts  0.73 us (2%)
    pallas_call x1, Pallas kernels, relay_call(): pl.pallas_call(functools.partial(relay_kernel, lon_count, lat_count), out...  30 us
    unnamed x1, local copies, waits for them, and re-layouts  0.73 us

commit v1 on v0

--- a/solution.py
+++ b/solution.py
@@ -294,11 +294,20 @@
     return min(lon_total // 2, 4 * row_total // min(row + 1, row_total - row))
 
 
+def fold_rows(lon_count, lat_count, rows, cols):
+    lon_total, row_total = lon_count * cols, lat_count * rows
+    fold = 2
+    while source_reach(lon_total, row_total, fold + 1) > 2 * cols:
+        fold += 2
+    return fold
+
+
 def relay_fits(lon_count, lat_count, rows, cols):
     lon_total, row_total = lon_count * cols, lat_count * rows
-    if lon_count != 8 or lat_count != 2 or rows % 8 != 0 or cols % 16 != 0:
+    if lon_count != 8 or lat_count != 2 or rows % 4 != 0 or cols != 16:
         return False
-    return source_reach(lon_total, row_total, rows // 2 + 1) <= cols and lon_total == 128
+    near = source_reach(lon_total, row_total, rows // 2 + 1) <= cols
+    return near and fold_rows(lon_count, lat_count, rows, cols) <= rows // 4
 
 
 def relay_kernel(
@@ -314,9 +323,13 @@
     down_hbm,
     out_ref,
     window,
+    fold_filters,
     wide_filters,
     near_filters,
     product,
+    mixed_ref,
+    fold_out,
+    fold_in,
     mix_ref,
     up_ref,
     down_ref,
@@ -329,13 +342,15 @@
     lon_total, row_total = lon_count * cols, lat_count * rows
     middle, part, half = lon_count // 2, cols // 2, rows // 2
     home = middle * cols
-    reaches = [source_reach(lon_total, row_total, p) for p in range(rows)]
-    full = sum(1 for r in reaches if r > 2 * cols)
+    fold = fold_rows(lon_count, lat_count, rows, cols)
+    reaches = [source_reach(lon_total, row_total, max(p, fold + 1)) for p in range(rows)]
     wide = sum(1 for r in reaches if r > cols + part)
     near = sum(1 for r in reaches if r > cols)
     me, lat = lax.axis_index("lon"), lax.axis_index("lat")
     north = lat == 0
     turn = 1 - 2 * lax.rem(me, 2)
+    place = lax.rem(me, middle)
+    inward = jnp.where(place < 2, 1, -1)
     edge = jnp.where(north, rows - 1, 0)
 
     def device(delta):
@@ -370,8 +385,18 @@
 
     outer, halo = jnp.where(north, 0, rows + 1), jnp.where(north, rows + 1, 0)
     clear(pl.ds(outer, 1), 0, lon_total)
-    clear(lines(full, wide), 0, home - 2 * cols)
-    clear(lines(full, wide), home + 3 * cols, lon_total)
+    clear(lines(fold + 1, wide), 0, home - 2 * cols)
+    clear(lines(fold + 1, wide), home + 3 * cols, lon_total)
+    clear(lines(fold - 1, fold + 1), 0, cols)
+
+    @pl.when(place != middle - 1)
+    def _():
+        clear(lines(fold - 1, fold + 1), cols, 2 * cols)
+
+    @pl.when(place != 0)
+    def _():
+        clear(lines(fold - 1, fold + 1), home + 3 * cols, lon_total)
+
     clear(lines(wide, near), 0, home - cols - part)
     clear(lines(wide, near), home + 2 * cols + part, lon_total)
     clear(lines(near, half + 1), 0, home - cols)
@@ -423,18 +448,26 @@
     after = pl.multiple_of(home + jnp.where(turn > 0, cols, -part), part)
     before = pl.multiple_of(home + jnp.where(turn > 0, -part, cols), part)
     near_cut = half + (rows - half) // 2
-    steps = (1, -1, 2)
     halo_own = to_core(home, cols)
     halo_across, halo_along = to_core(after, part), to_core(before, part)
-    across = [own_across(near_cut, rows), own_across(half, near_cut), own_across(wide, half)]
-    across_wide = own_across(0, wide)
-    along = [pass_along(near_cut, rows), pass_along(half, near_cut), pass_along(wide, half)]
+    cuts = [(near_cut, rows), (half - 1, near_cut), (wide - 1, half - 1)]
+    across = [own_across(*cut) for cut in cuts]
+    along = [pass_along(*cut) for cut in cuts[:2]] + [pass_along(wide, half - 1)]
     halves = [half_along(wide, near, e) for e in (1, -1)]
-    wide_along = {e: own_along(full, wide, e) for e in (1, -1)}
-    wide_across = message(lines(full, wide), at(2 * turn), at(turn), cols, partner)
-    bands = [(full - 1, full), (1, full - 1), (0, 1)]
-    full_along = [[own_along(a, b, e) for e in steps] for a, b in bands]
-    full_across = [[pass_across(a, b, e) for e in steps] for a, b in bands]
+    fold_own = own_across(0, fold + 1)
+    along_in, along_out = own_along(0, wide, inward), own_along(fold - 1, wide, -inward)
+    fold_across = pass_across(0, fold + 1, inward)
+    same = turn == inward
+    late_across = pass_across(fold + 1, wide, turn), pass_across(fold - 1, wide, turn)
+    index = count[0]
+    fold_swap = pltpu.make_async_remote_copy(
+        src_ref=fold_out,
+        dst_ref=fold_in,
+        send_sem=send_sem.at[index],
+        recv_sem=recv_sem.at[index],
+        device_id={"lon": device(middle)},
+        device_id_type=MESH,
+    )
 
     def start(*copies):
         for copy in copies:
@@ -463,9 +496,9 @@
     lanes = lax.broadcasted_iota(jnp.int32, (half, lon_total), 1)
     second = lax.rem(lax.broadcasted_iota(jnp.int32, (half, entries), 0), 2)
 
-    def turned(line):
+    def turned(line, shift):
         spread = jnp.broadcast_to(line, (cols, lon_total))
-        return pltpu.roll(spread, 0, 1, stride=1, stride_axis=0).astype(jnp.bfloat16)
+        return pltpu.roll(spread, shift, 1, stride=1, stride_axis=0)
 
     def build_near(k, carry):
         offset = table(lons_ref, k, half).astype(jnp.int32)
@@ -481,13 +514,18 @@
             for v in range(2):
                 spot_at = pl.multiple_of(k * 2 * cols + (n % 2) * cols, cols)
                 near_filters[n // 2, pl.ds(spot_at, cols), v * lon_total : (v + 1) * lon_total] = (
-                    turned(sums[v][n : n + 1, :])
+                    turned(sums[v][n : n + 1, :], 0).astype(jnp.bfloat16)
                 )
         return carry
 
-    def build_wide(k, carry):
-        spot = table(lons_ref, k, 0).astype(jnp.int32) + home
+    polar = lax.broadcasted_iota(jnp.int32, (half, entries), 0) < fold
+    start_col = jnp.where(polar, place * cols, home)
+    lower = lax.broadcasted_iota(jnp.int32, (cols, lon_total), 1) < home
+
+    def build_polar(k, carry):
+        spot = table(lons_ref, k, 0).astype(jnp.int32) + start_col
         spot = jnp.where(spot >= lon_total, spot - lon_total, spot)
+        spot = jnp.where(spot < 0, spot + lon_total, spot)
         row_offset = table(rows_ref, k, 0)
         weight = table(weights_ref, k, 0)
         picked = [jnp.where(row_offset == r, weight, 0.0) for r in (-1.0, 0.0, 1.0)]
@@ -496,16 +534,32 @@
             hit = spot[:, s : s + 1] == lanes
             for r in range(3):
                 sums[r] = sums[r] + jnp.where(hit, picked[r][:, s : s + 1], 0.0)
-        for n in range(half):
+        none = jnp.zeros((cols, lon_total), jnp.float32)
+        for n in range(fold):
+            late = n % 2
+            kept = [none] * 4
+            moved = [none] * 4
+            for r in range(3):
+                kept[r + late] = turned(sums[r][n : n + 1, :], 0)
+                moved[r + late] = turned(sums[r][n : n + 1, :], home)
+            for v in range(2):
+                here = jnp.where(lower, kept[2 * v], moved[2 * v + 1])
+                there = jnp.where(lower, moved[2 * v], kept[2 * v + 1])
+                for who, value in enumerate((here, there)):
+                    spot_at = pl.multiple_of(k * 4 * cols + (2 * who + late) * cols, cols)
+                    fold_filters[
+                        n // 2, pl.ds(spot_at, cols), v * lon_total : (v + 1) * lon_total
+                    ] = value.astype(jnp.bfloat16)
+        for n in range(fold, half):
             late = n % 2
             spot_at = pl.ds(pl.multiple_of(k * 2 * cols + late * cols, cols), cols)
             for r in range(3):
                 low = (r + late) * lon_total
-                wide_filters[n // 2, spot_at, low : low + lon_total] = turned(sums[r][n : n + 1, :])
+                wide_filters[(n - fold) // 2, spot_at, low : low + lon_total] = turned(
+                    sums[r][n : n + 1, :], 0
+                ).astype(jnp.bfloat16)
             low = (3 - 3 * late) * lon_total
-            wide_filters[n // 2, spot_at, low : low + lon_total] = jnp.zeros(
-                (cols, lon_total), jnp.bfloat16
-            )
+            wide_filters[(n - fold) // 2, spot_at, low : low + lon_total] = none.astype(jnp.bfloat16)
         return carry
 
     def filter_pairs(first, last):
@@ -520,7 +574,7 @@
                 matrix = near_filters[q - half // 2]
             else:
                 source = window[taken].reshape(4 * lon_total, channels)
-                matrix = wide_filters[q]
+                matrix = wide_filters[q - fold // 2]
             filtered = jnp.dot(matrix, source, preferred_element_type=jnp.float32)
             filtered = filtered.astype(jnp.bfloat16)
             for k in range(bases):
@@ -528,11 +582,32 @@
                     filtered[2 * k * cols : 2 * (k + 1) * cols]
                 )
 
-    def finish_pairs(first, last, between=()):
-        base = jnp.where(north, 2 * first, rows - 2 * last)
-        depth = 2 * (last - first)
+    def fold_pairs():
+        pairs = fold // 2
+        cells = fold * cols
+        base = jnp.where(north, 0, rows - fold)
+        for t in range(pairs):
+            q = jnp.where(north, t, pairs - 1 - t)
+            source = window[pl.ds(base + 2 * t, 4), pl.ds(at(-place), 4 * cols)]
+            source = source.reshape(16 * cols, channels)
+            filtered = jnp.dot(fold_filters[q], source, preferred_element_type=jnp.float32)
+            filtered = filtered.astype(jnp.bfloat16)
+            for k in range(bases):
+                for who in range(2):
+                    low, from_row = who * cells + 2 * t * cols, (4 * k + 2 * who) * cols
+                    product[low : low + 2 * cols, k * channels : (k + 1) * channels] = filtered[
+                        from_row : from_row + 2 * cols
+                    ]
+        mixed = jnp.dot(product[: 2 * cells], mix_ref[...], preferred_element_type=jnp.float32)
+        fold_out[...] = mixed[cells:].astype(jnp.bfloat16)
+        mixed_ref[pl.ds(jnp.where(north, 0, half * cols - cells), cells)] = mixed[:cells]
+
+    def mix_pairs(pairs):
+        cells = 2 * pairs * cols
+        return jnp.dot(product[:cells], mix_ref[...], preferred_element_type=jnp.float32)
+
+    def finish(mixed, base, depth):
         cells = depth * cols
-        mixed = jnp.dot(product[:cells], mix_ref[...], preferred_element_type=jnp.float32)
         here = window[pl.ds(base + 1, depth), home : home + cols].reshape(cells, channels)
         latent = here.astype(jnp.float32) + mixed
         mean = jnp.mean(latent, axis=1, keepdims=True)
@@ -549,51 +624,68 @@
         result = (latent + lowered).astype(jnp.bfloat16)
         out_ref[pl.ds(base, depth)] = result.reshape(depth, cols, channels)
 
+    fold_pair, half_pair, all_pairs = fold // 2, half // 2, rows // 2
     pl.semaphore_wait(barrier, len(others))
     fetch.wait()
-    start(halo_own, *across, across_wide)
-    start(*wide_along.values(), *full_along[0])
+    start(halo_own, fold_own, along_in, along_out, across[0], across[1], *halves)
     lax.fori_loop(0, bases, build_near, 0)
+    lax.fori_loop(0, bases, build_polar, 0)
     arrived(across[0])
     start(along[0], halo_across)
-    start(*full_along[1])
-    lax.fori_loop(0, bases, build_wide, 0)
+    arrived(along_in)
+    start(fold_across, across[2])
     arrived(across[1])
     start(along[1])
-    arrived(*wide_along.values())
-    start(wide_across)
-    arrived(*full_along[0])
-    start(*full_across[0])
-    start(*full_along[2])
+    arrived(along_out)
+
+    @pl.when(same)
+    def _():
+        start(late_across[0])
+
+    @pl.when(jnp.logical_not(same))
+    def _():
+        start(late_across[1])
+
+    for load in loads:
+        load.wait()
+    arrived(fold_own, fold_across)
+    fold_pairs()
     arrived(across[2])
-    start(along[2], *halves)
+    start(along[2])
+    start(fold_swap)
     arrived(along[0])
     start(halo_along)
-    for load in loads:
-        load.wait()
-    quarter = half // 4
-    arrived(halo_own, halo_across, halo_along)
-    arrived(*full_along[1])
-    start(*full_across[1])
-    arrived(along[1])
-    filter_pairs(3 * quarter, 4 * quarter)
-    finish_pairs(3 * quarter, 4 * quarter)
-    arrived(*full_along[2])
-    start(*full_across[2])
-    arrived(along[2], *halves)
-    filter_pairs(2 * quarter, 3 * quarter)
-    finish_pairs(2 * quarter, 3 * quarter)
-    arrived(across_wide, wide_across, *full_across[0])
-    filter_pairs(quarter, 2 * quarter)
-    finish_pairs(quarter, 2 * quarter)
-    arrived(*full_across[1], *full_across[2])
-    filter_pairs(0, quarter)
-    finish_pairs(0, quarter)
-    sent = [halo_own, halo_across, halo_along, across_wide, wide_across]
-    sent += across + along + halves + list(wide_along.values())
-    for group in full_along + full_across:
-        sent += group
-    for copy in sent:
+    arrived(halo_own, halo_across, halo_along, along[1], *halves)
+    filter_pairs(half_pair, all_pairs)
+    finish(mix_pairs(all_pairs - half_pair), jnp.where(north, half, 0), rows - half)
+    arrived(along[2])
+
+    @pl.when(same)
+    def _():
+        arrived(late_across[1])
+
+    @pl.when(jnp.logical_not(same))
+    def _():
+        arrived(late_across[0])
+
+    filter_pairs(fold_pair, half_pair)
+    cells = (half - fold) * cols
+    mixed_ref[pl.ds(jnp.where(north, fold * cols, 0), cells)] = mix_pairs(half_pair - fold_pair)
+    arrived(fold_swap)
+    own_part = pl.ds(jnp.where(north, 0, half * cols - fold * cols), fold * cols)
+    mixed_ref[own_part] = mixed_ref[own_part] + fold_in[...].astype(jnp.float32)
+    finish(mixed_ref[...], jnp.where(north, 0, half), half)
+
+    @pl.when(same)
+    def _():
+        late_across[0].wait_send()
+
+    @pl.when(jnp.logical_not(same))
+    def _():
+        late_across[1].wait_send()
+
+    sent = [halo_own, halo_across, halo_along, fold_own, fold_across, along_in, along_out]
+    for copy in sent + across + along + halves + [fold_swap]:
         copy.wait_send()
 
 
@@ -612,7 +704,8 @@
     channels, rows, cols = fields.shape
     bases, hidden = mix_weight.shape[0], up_weight.shape[1]
     lon_total = lon_count * cols
-    half, copies = rows // 2, 36
+    half, copies = rows // 2, 20
+    fold = fold_rows(lon_count, lat_count, rows, cols)
     in_vmem = pl.BlockSpec(memory_space=pltpu.VMEM)
     anywhere = pl.BlockSpec(memory_space=pl.ANY)
     result = pl.pallas_call(
@@ -622,9 +715,13 @@
         out_specs=in_vmem,
         scratch_shapes=[
             pltpu.VMEM((rows + 2, lon_total, channels), jnp.bfloat16),
-            pltpu.VMEM((half // 2, 2 * bases * cols, 4 * lon_total), jnp.bfloat16),
+            pltpu.VMEM((fold // 2, 4 * bases * cols, 16 * cols), jnp.bfloat16),
+            pltpu.VMEM(((half - fold) // 2, 2 * bases * cols, 4 * lon_total), jnp.bfloat16),
             pltpu.VMEM((half // 2, 2 * bases * cols, 16 * cols), jnp.bfloat16),
             pltpu.VMEM((half * cols, bases * channels), jnp.bfloat16),
+            pltpu.VMEM((half * cols, channels), jnp.float32),
+            pltpu.VMEM((fold * cols, channels), jnp.bfloat16),
+            pltpu.VMEM((fold * cols, channels), jnp.bfloat16),
             pltpu.VMEM((bases * channels, channels), jnp.bfloat16),
             pltpu.VMEM((channels, hidden), jnp.bfloat16),
             pltpu.VMEM((hidden, channels), jnp.bfloat16),

time: 30.9 us -> 25.4 us (0.82)
  Pallas kernels: 30 us -> 24.3 us
    pallas_call x1, Pallas kernels: 30 us -> 24.3 us  [relay_call(): pl.pallas_call(functools.partial(relay_kernel, lon_count, lat_count), out...]
where the time goes in v1:
time: 25.4 us; the launch traced here: 25 us
  Pallas kernels  24.3 us (96%)
  local copies, waits for them, and re-layouts  0.73 us (3%)
    pallas_call x1, Pallas kernels, relay_call(): pl.pallas_call(functools.partial(relay_kernel, lon_count, lat_count), out...  24.3 us
    unnamed x1, local copies, waits for them, and re-layouts  0.73 us

profile of v1, /device:TPU:0, one launch (start us, length us, event | category | flops | bytes accessed | tf_op | source)
XLA Modules:
  0.0 25.0 jit_solution(18043577479787722303)
XLA Ops:
  0.0 24.3 %shard_map.82 = bf16[16,16,640]{2,1,0:T(8,128)(2,1)S(1)} custom-call(bf16[16,16,640]{2,1,0:T(8,128)(2,1)} %bitcast.8, s32[7,16,32]{2,1,0:T(8,128)} %bitcast.9, s32[7,16,32]{2,1,0:T(8,128)} %bitcast.10, f32[7,16,32]{2,1,0:T(8,128)} %bitcast.11, f32[640]{0:T(1024)} %gain_ref.1, bf16[4480,640]{1,0:T(8,128)(2,1)} %bitcast.7, bf16[640,1280]{1,0:T(8,128)(2,1)} %up_hbm.1, ...), custom_call_target="tpu_custom_call" | custom-call | tf_op jit(solution)/shard_map/pallas_call | solution.py:711
  24.3 0.7 %copy.10 = bf16[640,16,16]{0,2,1:T(8,128)(2,1)} copy(bf16[640,16,16]{0,2,1:T(8,128)(2,1)S(1)} %bitcast.6) | data formatting | bytes 655360

commit v2 on v1

--- a/solution.py
+++ b/solution.py
@@ -336,6 +336,8 @@
     send_sem,
     recv_sem,
     load_sem,
+    ready,
+    tables,
 ):
     rows, cols, channels = x_hbm.shape
     bases, entries = rows_ref.shape[:2]
@@ -372,10 +374,24 @@
         pltpu.make_async_copy(down_hbm, down_ref, load_sem.at[2]),
     ]
     barrier = pltpu.get_barrier_semaphore()
-    others = [{"lon": me + turn}] + [{"lon": device(2 * e)} for e in (1, -1, 2)]
-    others.append({"lat": 1 - lat})
-    for other in others:
-        pl.semaphore_signal(barrier, inc=1, device_id=other, device_id_type=MESH)
+    above, below = me < lon_count - 2, me >= 2
+    inner = jnp.logical_and(above, below)
+    outer = jnp.logical_not(inner)
+
+    def greet(semaphore, **other):
+        pl.semaphore_signal(semaphore, inc=1, device_id=other, device_id_type=MESH)
+
+    greet(barrier, lon=me + turn)
+    greet(barrier, lat=1 - lat)
+
+    @pl.when(above)
+    def _():
+        greet(barrier, lon=me + 2)
+
+    @pl.when(below)
+    def _():
+        greet(barrier, lon=me - 2)
+
     for load in loads:
         load.start()
 
@@ -383,8 +399,9 @@
         size = where.size if isinstance(where, pl.Slice) else 1
         window[where, low:high] = jnp.zeros((size, high - low, channels), jnp.bfloat16)
 
-    outer, halo = jnp.where(north, 0, rows + 1), jnp.where(north, rows + 1, 0)
-    clear(pl.ds(outer, 1), 0, lon_total)
+    near_cut = half + (rows - half) // 2
+    sky, halo = jnp.where(north, 0, rows + 1), jnp.where(north, rows + 1, 0)
+    clear(pl.ds(sky, 1), 0, lon_total)
     clear(lines(fold + 1, wide), 0, home - 2 * cols)
     clear(lines(fold + 1, wide), home + 3 * cols, lon_total)
     clear(lines(fold - 1, fold + 1), 0, cols)
@@ -401,9 +418,29 @@
     clear(lines(wide, near), home + 2 * cols + part, lon_total)
     clear(lines(near, half + 1), 0, home - cols)
     clear(lines(near, half + 1), home + 2 * cols, lon_total)
-    clear(lines(half + 1, rows), home + 2 * cols, home + 3 * cols)
+    clear(lines(half + 1, near_cut), home + 2 * cols, home + 3 * cols)
+
+    @pl.when(turn < 0)
+    def _():
+        clear(lines(near_cut, rows), home + 2 * cols, home + 3 * cols)
+
     clear(pl.ds(halo, 1), home - cols, home - part)
     clear(pl.ds(halo, 1), home + cols + part, home + 3 * cols)
+
+    span = (rows, rows_ref.shape[2])
+    order = lax.broadcasted_iota(jnp.int32, span, 0)
+    local = jnp.where(north, order, rows - 2 - order + 2 * lax.rem(order, 2))
+    mine = (local + lat * rows == lax.broadcasted_iota(jnp.int32, span, 1)).astype(jnp.float32)
+    for which, ref in enumerate((rows_ref, lons_ref, weights_ref)):
+        own = lax.dot_general(
+            mine,
+            ref[...].astype(jnp.float32).reshape(bases * entries, rows_ref.shape[2]),
+            (((1,), (1,)), ((), ())),
+            precision=lax.Precision.HIGHEST,
+            preferred_element_type=jnp.float32,
+        )
+        for k in range(bases):
+            tables[which, k] = own[:, k * entries : (k + 1) * entries]
 
     count = [0]
 
@@ -447,14 +484,14 @@
 
     after = pl.multiple_of(home + jnp.where(turn > 0, cols, -part), part)
     before = pl.multiple_of(home + jnp.where(turn > 0, -part, cols), part)
-    near_cut = half + (rows - half) // 2
     halo_own = to_core(home, cols)
     halo_across, halo_along = to_core(after, part), to_core(before, part)
-    cuts = [(near_cut, rows), (half - 1, near_cut), (wide - 1, half - 1)]
-    across = [own_across(*cut) for cut in cuts]
-    along = [pass_along(*cut) for cut in cuts[:2]] + [pass_along(wide, half - 1)]
+    across = [own_across(near_cut, rows), own_across(wide, near_cut)]
+    along = pass_along(wide, near_cut)
+    direct = own_along(near_cut, rows, -turn)
+    direct_across = pass_across(near_cut, rows, turn)
     halves = [half_along(wide, near, e) for e in (1, -1)]
-    fold_own = own_across(0, fold + 1)
+    fold_own = own_across(0, wide)
     along_in, along_out = own_along(0, wide, inward), own_along(fold - 1, wide, -inward)
     fold_across = pass_across(0, fold + 1, inward)
     same = turn == inward
@@ -477,22 +514,6 @@
         for copy in copies:
             copy.wait_recv()
 
-    wide_rows = (half, rows_ref.shape[2])
-
-    def table(ref, k, first):
-        order = lax.broadcasted_iota(jnp.int32, wide_rows, 0) + first
-        local = jnp.where(north, order, rows - 2 - order + 2 * lax.rem(order, 2))
-        mine = (local + lat * rows == lax.broadcasted_iota(jnp.int32, wide_rows, 1)).astype(
-            jnp.float32
-        )
-        return lax.dot_general(
-            mine,
-            ref[k].astype(jnp.float32),
-            (((1,), (1,)), ((), ())),
-            precision=lax.Precision.HIGHEST,
-            preferred_element_type=jnp.float32,
-        )
-
     lanes = lax.broadcasted_iota(jnp.int32, (half, lon_total), 1)
     second = lax.rem(lax.broadcasted_iota(jnp.int32, (half, entries), 0), 2)
 
@@ -501,9 +522,9 @@
         return pltpu.roll(spread, shift, 1, stride=1, stride_axis=0)
 
     def build_near(k, carry):
-        offset = table(lons_ref, k, half).astype(jnp.int32)
-        row_offset = table(rows_ref, k, half).astype(jnp.int32)
-        weight = table(weights_ref, k, half)
+        offset = tables[1, k, half:].astype(jnp.int32)
+        row_offset = tables[0, k, half:].astype(jnp.int32)
+        weight = tables[2, k, half:]
         spot = (row_offset + 1 + second) * (4 * cols) + offset + cols
         sums = [jnp.zeros((half, lon_total), jnp.float32) for _ in range(2)]
         for s in range(entries):
@@ -523,11 +544,11 @@
     lower = lax.broadcasted_iota(jnp.int32, (cols, lon_total), 1) < home
 
     def build_polar(k, carry):
-        spot = table(lons_ref, k, 0).astype(jnp.int32) + start_col
+        spot = tables[1, k, :half].astype(jnp.int32) + start_col
         spot = jnp.where(spot >= lon_total, spot - lon_total, spot)
         spot = jnp.where(spot < 0, spot + lon_total, spot)
-        row_offset = table(rows_ref, k, 0)
-        weight = table(weights_ref, k, 0)
+        row_offset = tables[0, k, :half]
+        weight = tables[2, k, :half]
         picked = [jnp.where(row_offset == r, weight, 0.0) for r in (-1.0, 0.0, 1.0)]
         sums = [jnp.zeros((half, lon_total), jnp.float32) for _ in range(3)]
         for s in range(entries):
@@ -625,40 +646,75 @@
         out_ref[pl.ds(base, depth)] = result.reshape(depth, cols, channels)
 
     fold_pair, half_pair, all_pairs = fold // 2, half // 2, rows // 2
-    pl.semaphore_wait(barrier, len(others))
+    pl.semaphore_wait(barrier, 2 + jnp.where(above, 1, 0) + jnp.where(below, 1, 0))
+
+    @pl.when(inner)
+    def _():
+        greet(ready.at[0], lon=me + 2)
+        greet(ready.at[0], lon=me - 2)
+
     fetch.wait()
-    start(halo_own, fold_own, along_in, along_out, across[0], across[1], *halves)
-    lax.fori_loop(0, bases, build_near, 0)
-    lax.fori_loop(0, bases, build_polar, 0)
-    arrived(across[0])
-    start(along[0], halo_across)
+    start(halo_own, fold_own, along_in, across[1])
+    goes_near = jnp.logical_or(inner, jnp.logical_not(same))
+
+    @pl.when(goes_near)
+    def _():
+        start(direct)
+
+    @pl.when(inner)
+    def _():
+        start(along_out)
+
+    lax.fori_loop(0, bases // 2, build_near, 0)
+    pl.semaphore_wait(ready.at[0], 1)
+
+    @pl.when(inner)
+    def _():
+        greet(ready.at[1], lon=device(2 * inward))
+
+    lax.fori_loop(bases // 2, bases, build_near, 0)
+    lax.fori_loop(0, bases // 2, build_polar, 0)
+
+    @pl.when(outer)
+    def _():
+        pl.semaphore_wait(ready.at[1], 1)
+
+        @pl.when(same)
+        def _():
+            start(direct)
+
+        start(along_out)
+
+    start(*halves)
+    lax.fori_loop(bases // 2, bases, build_polar, 0)
     arrived(along_in)
-    start(fold_across, across[2])
+    start(fold_across, across[0])
     arrived(across[1])
-    start(along[1])
-    arrived(along_out)
-
-    @pl.when(same)
-    def _():
-        start(late_across[0])
-
-    @pl.when(jnp.logical_not(same))
-    def _():
-        start(late_across[1])
-
+    start(along)
+    arrived(direct)
+    start(direct_across)
     for load in loads:
         load.wait()
     arrived(fold_own, fold_across)
     fold_pairs()
-    arrived(across[2])
-    start(along[2])
+    arrived(along_out)
+
+    @pl.when(same)
+    def _():
+        start(late_across[0])
+
+    @pl.when(jnp.logical_not(same))
+    def _():
+        start(late_across[1])
+
     start(fold_swap)
-    arrived(along[0])
+    arrived(across[0])
+    start(halo_across)
+    arrived(direct_across)
     start(halo_along)
-    arrived(halo_own, halo_across, halo_along, along[1], *halves)
+    arrived(halo_own, halo_across, halo_along, along, *halves)
     filter_pairs(half_pair, all_pairs)
     finish(mix_pairs(all_pairs - half_pair), jnp.where(north, half, 0), rows - half)
-    arrived(along[2])
 
     @pl.when(same)
     def _():
@@ -685,7 +741,8 @@
         late_across[1].wait_send()
 
     sent = [halo_own, halo_across, halo_along, fold_own, fold_across, along_in, along_out]
-    for copy in sent + across + along + halves + [fold_swap]:
+    sent += [along, direct, direct_across, fold_swap]
+    for copy in sent + across + halves:
         copy.wait_send()
 
 
@@ -728,6 +785,8 @@
             pltpu.SemaphoreType.DMA((copies,)),
             pltpu.SemaphoreType.DMA((copies,)),
             pltpu.SemaphoreType.DMA((4,)),
+            pltpu.SemaphoreType.REGULAR((2,)),
+            pltpu.VMEM((3, bases, rows, support_rows.shape[2]), jnp.float32),
         ],
         compiler_params=pltpu.CompilerParams(
             collective_id=0, has_side_effects=True, vmem_limit_bytes=56 * 1024 * 1024

time: 25.4 us -> 24.4 us (0.961)
  Pallas kernels: 24.3 us -> 23.5 us
    pallas_call x1, Pallas kernels: 24.3 us -> 23.5 us  [relay_call(): pl.pallas_call(functools.partial(relay_kernel, lon_count, lat_count), out...]
where the time goes in v2:
time: 24.4 us; the launch traced here: 24.2 us
  Pallas kernels  23.5 us (96%)
  local copies, waits for them, and re-layouts  0.73 us (3%)
    pallas_call x1, Pallas kernels, relay_call(): pl.pallas_call(functools.partial(relay_kernel, lon_count, lat_count), out...  23.5 us
    unnamed x1, local copies, waits for them, and re-layouts  0.73 us

profile of v2, /device:TPU:0, one launch (start us, length us, event | category | flops | bytes accessed | tf_op | source)
XLA Modules:
  0.0 24.2 jit_solution(16133192547180452688)
XLA Ops:
  0.0 23.5 %shard_map.82 = bf16[16,16,640]{2,1,0:T(8,128)(2,1)S(1)} custom-call(bf16[16,16,640]{2,1,0:T(8,128)(2,1)} %bitcast.8, s32[7,16,32]{2,1,0:T(8,128)} %bitcast.9, s32[7,16,32]{2,1,0:T(8,128)} %bitcast.10, f32[7,16,32]{2,1,0:T(8,128)} %bitcast.11, f32[640]{0:T(1024)} %gain_ref.1, bf16[4480,640]{1,0:T(8,128)(2,1)} %bitcast.7, bf16[640,1280]{1,0:T(8,128)(2,1)} %up_hbm.1, ...), custom_call_target="tpu_custom_call" | custom-call | tf_op jit(solution)/shard_map/pallas_call | solution.py:768
  23.5 0.7 %copy.10 = bf16[640,16,16]{0,2,1:T(8,128)(2,1)} copy(bf16[640,16,16]{0,2,1:T(8,128)(2,1)S(1)} %bitcast.6) | data formatting | bytes 655360

commit v3 on v2

--- a/solution.py
+++ b/solution.py
@@ -314,10 +314,10 @@
     lon_count,
     lat_count,
     x_hbm,
-    rows_ref,
-    lons_ref,
-    weights_ref,
-    gain_ref,
+    rows_hbm,
+    lons_hbm,
+    weights_hbm,
+    gain_hbm,
     mix_hbm,
     up_hbm,
     down_hbm,
@@ -328,8 +328,10 @@
     near_filters,
     product,
     mixed_ref,
-    fold_out,
-    fold_in,
+    fold_out_a,
+    fold_out_b,
+    fold_in_a,
+    fold_in_b,
     mix_ref,
     up_ref,
     down_ref,
@@ -338,6 +340,10 @@
     load_sem,
     ready,
     tables,
+    rows_ref,
+    lons_ref,
+    weights_ref,
+    gain_ref,
 ):
     rows, cols, channels = x_hbm.shape
     bases, entries = rows_ref.shape[:2]
@@ -367,12 +373,18 @@
     fetch = pltpu.make_async_copy(
         x_hbm, window.at[pl.ds(1, rows), pl.ds(home, cols)], load_sem.at[3]
     )
-    fetch.start()
     loads = [
         pltpu.make_async_copy(mix_hbm, mix_ref, load_sem.at[0]),
         pltpu.make_async_copy(up_hbm, up_ref, load_sem.at[1]),
         pltpu.make_async_copy(down_hbm, down_ref, load_sem.at[2]),
     ]
+    supports = [
+        pltpu.make_async_copy(source, landing, load_sem.at[4 + n])
+        for n, (source, landing) in enumerate(
+            [(rows_hbm, rows_ref), (lons_hbm, lons_ref), (weights_hbm, weights_ref)]
+        )
+    ]
+    loads.append(pltpu.make_async_copy(gain_hbm, gain_ref, load_sem.at[7]))
     barrier = pltpu.get_barrier_semaphore()
     above, below = me < lon_count - 2, me >= 2
     inner = jnp.logical_and(above, below)
@@ -392,14 +404,14 @@
     def _():
         greet(barrier, lon=me - 2)
 
-    for load in loads:
+    for load in [fetch] + supports + loads:
         load.start()
 
     def clear(where, low, high):
         size = where.size if isinstance(where, pl.Slice) else 1
         window[where, low:high] = jnp.zeros((size, high - low, channels), jnp.bfloat16)
 
-    near_cut = half + (rows - half) // 2
+    near_cut, last = half + (rows - half) // 2 - 1, rows - 1
     sky, halo = jnp.where(north, 0, rows + 1), jnp.where(north, rows + 1, 0)
     clear(pl.ds(sky, 1), 0, lon_total)
     clear(lines(fold + 1, wide), 0, home - 2 * cols)
@@ -419,14 +431,17 @@
     clear(lines(near, half + 1), 0, home - cols)
     clear(lines(near, half + 1), home + 2 * cols, lon_total)
     clear(lines(half + 1, near_cut), home + 2 * cols, home + 3 * cols)
+    clear(lines(last, rows), home + 2 * cols, home + 3 * cols)
 
     @pl.when(turn < 0)
     def _():
-        clear(lines(near_cut, rows), home + 2 * cols, home + 3 * cols)
+        clear(lines(near_cut, last), home + 2 * cols, home + 3 * cols)
 
     clear(pl.ds(halo, 1), home - cols, home - part)
     clear(pl.ds(halo, 1), home + cols + part, home + 3 * cols)
 
+    for support in supports:
+        support.wait()
     span = (rows, rows_ref.shape[2])
     order = lax.broadcasted_iota(jnp.int32, span, 0)
     local = jnp.where(north, order, rows - 2 - order + 2 * lax.rem(order, 2))
@@ -486,25 +501,30 @@
     before = pl.multiple_of(home + jnp.where(turn > 0, -part, cols), part)
     halo_own = to_core(home, cols)
     halo_across, halo_along = to_core(after, part), to_core(before, part)
-    across = [own_across(near_cut, rows), own_across(wide, near_cut)]
-    along = pass_along(wide, near_cut)
-    direct = own_along(near_cut, rows, -turn)
-    direct_across = pass_across(near_cut, rows, turn)
+    across = [own_across(last, rows), own_across(wide, near_cut)]
+    across_late = [own_across(fold + 1, wide), own_across(near_cut, last)]
+    along = [pass_along(last, rows), pass_along(wide, near_cut)]
+    direct = own_along(near_cut, last, -turn)
+    direct_across = pass_across(near_cut, last, turn)
     halves = [half_along(wide, near, e) for e in (1, -1)]
-    fold_own = own_across(0, wide)
+    fold_own = own_across(0, fold + 1)
     along_in, along_out = own_along(0, wide, inward), own_along(fold - 1, wide, -inward)
     fold_across = pass_across(0, fold + 1, inward)
     same = turn == inward
     late_across = pass_across(fold + 1, wide, turn), pass_across(fold - 1, wide, turn)
-    index = count[0]
-    fold_swap = pltpu.make_async_remote_copy(
-        src_ref=fold_out,
-        dst_ref=fold_in,
-        send_sem=send_sem.at[index],
-        recv_sem=recv_sem.at[index],
-        device_id={"lon": device(middle)},
-        device_id_type=MESH,
-    )
+    pieces = channels // 256 // 2 * 256
+    pieces = [(0, pieces), (pieces, channels)]
+    fold_swap = [
+        pltpu.make_async_remote_copy(
+            src_ref=(fold_out_a, fold_out_b)[n],
+            dst_ref=(fold_in_a, fold_in_b)[n],
+            send_sem=send_sem.at[count[0] + n],
+            recv_sem=recv_sem.at[count[0] + n],
+            device_id={"lon": device(middle)},
+            device_id_type=MESH,
+        )
+        for n, (low, high) in enumerate(pieces)
+    ]
 
     def start(*copies):
         for copy in copies:
@@ -619,9 +639,14 @@
                     product[low : low + 2 * cols, k * channels : (k + 1) * channels] = filtered[
                         from_row : from_row + 2 * cols
                     ]
-        mixed = jnp.dot(product[: 2 * cells], mix_ref[...], preferred_element_type=jnp.float32)
-        fold_out[...] = mixed[cells:].astype(jnp.bfloat16)
-        mixed_ref[pl.ds(jnp.where(north, 0, half * cols - cells), cells)] = mixed[:cells]
+
+    def fold_mix(low, high):
+        cells = fold * cols
+        mixed = jnp.dot(
+            product[: 2 * cells], mix_ref[:, low:high], preferred_element_type=jnp.float32
+        )
+        (fold_out_a if low == 0 else fold_out_b)[...] = mixed[cells:].astype(jnp.bfloat16)
+        mixed_ref[pl.ds(jnp.where(north, 0, half * cols - cells), cells), low:high] = mixed[:cells]
 
     def mix_pairs(pairs):
         cells = 2 * pairs * cols
@@ -654,7 +679,7 @@
         greet(ready.at[0], lon=me - 2)
 
     fetch.wait()
-    start(halo_own, fold_own, along_in, across[1])
+    start(halo_own, *across, fold_own, along_in)
     goes_near = jnp.logical_or(inner, jnp.logical_not(same))
 
     @pl.when(goes_near)
@@ -688,15 +713,18 @@
     start(*halves)
     lax.fori_loop(bases // 2, bases, build_polar, 0)
     arrived(along_in)
-    start(fold_across, across[0])
-    arrived(across[1])
-    start(along)
+    start(fold_across, *across_late)
+    arrived(*across)
+    start(*along, halo_across)
     arrived(direct)
     start(direct_across)
     for load in loads:
         load.wait()
     arrived(fold_own, fold_across)
     fold_pairs()
+    for swap, (low, high) in zip(fold_swap, pieces):
+        fold_mix(low, high)
+        start(swap)
     arrived(along_out)
 
     @pl.when(same)
@@ -707,12 +735,9 @@
     def _():
         start(late_across[1])
 
-    start(fold_swap)
-    arrived(across[0])
-    start(halo_across)
-    arrived(direct_across)
+    arrived(along[0])
     start(halo_along)
-    arrived(halo_own, halo_across, halo_along, along, *halves)
+    arrived(across_late[1], direct_across, halo_own, halo_across, halo_along, along[1], *halves)
     filter_pairs(half_pair, all_pairs)
     finish(mix_pairs(all_pairs - half_pair), jnp.where(north, half, 0), rows - half)
 
@@ -724,12 +749,14 @@
     def _():
         arrived(late_across[0])
 
+    arrived(across_late[0])
     filter_pairs(fold_pair, half_pair)
     cells = (half - fold) * cols
     mixed_ref[pl.ds(jnp.where(north, fold * cols, 0), cells)] = mix_pairs(half_pair - fold_pair)
-    arrived(fold_swap)
+    arrived(*fold_swap)
     own_part = pl.ds(jnp.where(north, 0, half * cols - fold * cols), fold * cols)
-    mixed_ref[own_part] = mixed_ref[own_part] + fold_in[...].astype(jnp.float32)
+    for (low, high), piece in zip(pieces, (fold_in_a, fold_in_b)):
+        mixed_ref[own_part, low:high] = mixed_ref[own_part, low:high] + piece[...].astype(jnp.float32)
     finish(mixed_ref[...], jnp.where(north, 0, half), half)
 
     @pl.when(same)
@@ -741,8 +768,8 @@
         late_across[1].wait_send()
 
     sent = [halo_own, halo_across, halo_along, fold_own, fold_across, along_in, along_out]
-    sent += [along, direct, direct_across, fold_swap]
-    for copy in sent + across + halves:
+    sent += [direct, direct_across] + fold_swap
+    for copy in sent + across + across_late + along + halves:
         copy.wait_send()
 
 
@@ -761,14 +788,15 @@
     channels, rows, cols = fields.shape
     bases, hidden = mix_weight.shape[0], up_weight.shape[1]
     lon_total = lon_count * cols
-    half, copies = rows // 2, 20
+    half, copies = rows // 2, 24
     fold = fold_rows(lon_count, lat_count, rows, cols)
+    piece = channels // 256 // 2 * 256
     in_vmem = pl.BlockSpec(memory_space=pltpu.VMEM)
     anywhere = pl.BlockSpec(memory_space=pl.ANY)
     result = pl.pallas_call(
         functools.partial(relay_kernel, lon_count, lat_count),
         out_shape=pltpu.VMEM((rows, cols, channels), jnp.bfloat16),
-        in_specs=[anywhere] + [in_vmem] * 4 + [anywhere] * 3,
+        in_specs=[anywhere] * 8,
         out_specs=in_vmem,
         scratch_shapes=[
             pltpu.VMEM((rows + 2, lon_total, channels), jnp.bfloat16),
@@ -777,16 +805,22 @@
             pltpu.VMEM((half // 2, 2 * bases * cols, 16 * cols), jnp.bfloat16),
             pltpu.VMEM((half * cols, bases * channels), jnp.bfloat16),
             pltpu.VMEM((half * cols, channels), jnp.float32),
-            pltpu.VMEM((fold * cols, channels), jnp.bfloat16),
-            pltpu.VMEM((fold * cols, channels), jnp.bfloat16),
+            pltpu.VMEM((fold * cols, piece), jnp.bfloat16),
+            pltpu.VMEM((fold * cols, channels - piece), jnp.bfloat16),
+            pltpu.VMEM((fold * cols, piece), jnp.bfloat16),
+            pltpu.VMEM((fold * cols, channels - piece), jnp.bfloat16),
             pltpu.VMEM((bases * channels, channels), jnp.bfloat16),
             pltpu.VMEM((channels, hidden), jnp.bfloat16),
             pltpu.VMEM((hidden, channels), jnp.bfloat16),
             pltpu.SemaphoreType.DMA((copies,)),
             pltpu.SemaphoreType.DMA((copies,)),
-            pltpu.SemaphoreType.DMA((4,)),
+            pltpu.SemaphoreType.DMA((8,)),
             pltpu.SemaphoreType.REGULAR((2,)),
             pltpu.VMEM((3, bases, rows, support_rows.shape[2]), jnp.float32),
+            pltpu.VMEM((bases, support_rows.shape[2], support_rows.shape[1]), jnp.int32),
+            pltpu.VMEM((bases, support_rows.shape[2], support_rows.shape[1]), jnp.int32),
+            pltpu.VMEM((bases, support_rows.shape[2], support_rows.shape[1]), jnp.float32),
+            pltpu.VMEM((channels,), jnp.float32),
         ],
         compiler_params=pltpu.CompilerParams(
             collective_id=0, has_side_effects=True, vmem_limit_bytes=56 * 1024 * 1024

time: 24.4 us -> 22.8 us (0.934)
  Pallas kernels: 23.5 us -> 21.9 us
    pallas_call x1, Pallas kernels: 23.5 us -> 21.9 us  [relay_call(): pl.pallas_call(functools.partial(relay_kernel, lon_count, lat_count), out...]
where the time goes in v3:
time: 22.8 us; the launch traced here: 22.7 us
  Pallas kernels  21.9 us (96%)
  local copies, waits for them, and re-layouts  0.73 us (3%)
    pallas_call x1, Pallas kernels, relay_call(): pl.pallas_call(functools.partial(relay_kernel, lon_count, lat_count), out...  21.9 us
    unnamed x1, local copies, waits for them, and re-layouts  0.73 us

profile of v3, /device:TPU:0, one launch (start us, length us, event | category | flops | bytes accessed | tf_op | source)
XLA Modules:
  0.0 22.7 jit_solution(793163297662662565)
XLA Ops:
  0.0 21.9 %shard_map.82 = bf16[16,16,640]{2,1,0:T(8,128)(2,1)S(1)} custom-call(bf16[16,16,640]{2,1,0:T(8,128)(2,1)} %bitcast.8, s32[7,16,32]{2,1,0:T(8,128)} %bitcast.9, s32[7,16,32]{2,1,0:T(8,128)} %bitcast.10, f32[7,16,32]{2,1,0:T(8,128)} %bitcast.11, f32[640]{0:T(1024)} %gain_hbm.1, bf16[4480,640]{1,0:T(8,128)(2,1)} %bitcast.7, bf16[640,1280]{1,0:T(8,128)(2,1)} %up_hbm.1, ...), custom_call_target="tpu_custom_call" | custom-call | tf_op jit(solution)/shard_map/pallas_call | solution.py:796
  21.9 0.7 %copy.10 = bf16[640,16,16]{0,2,1:T(8,128)(2,1)} copy(bf16[640,16,16]{0,2,1:T(8,128)(2,1)S(1)} %bitcast.6) | data formatting | bytes 655360
